TPU v7x, 32 devices: a whole 2x2x4 slice. The times are simulated.
32 devices in a mesh: groups: 2 (over x), ctx: 8 (over z, y), head: 2 (over core).
Axes of the slice: x: 2, y: 2, z: 4, core: 2. Of those that a mesh axis runs over, the one named last changes fastest.
Arguments:
- queries: bfloat16 [2, 256, 64, 128], P('groups', 'ctx', 'head'), parts along dimension 0, may hold values from -400 to 400
- new_keys: bfloat16 [2, 256, 8, 128], P('groups', 'ctx', 'head'), parts along dimension 0, may hold values from -5 to 5
- new_values: bfloat16 [2, 256, 8, 128], P('groups', 'ctx', 'head'), parts along dimension 0, may hold values from -6 to 6
- history_keys: bfloat16 [2, 8192, 8, 128], P('groups', 'ctx', 'head'), parts along dimension 0, may hold values from -6 to 6
- history_values: bfloat16 [2, 8192, 8, 128], P('groups', 'ctx', 'head'), parts along dimension 0, may hold values from -6 to 6
- block_mask: int32 [2, 2, 64], P('groups', None, 'ctx'), parts along dimension 0, may hold values from 0 to 1, as said below
Outputs:
- attended: bfloat16 [2, 256, 64, 128], P('groups', 'ctx', 'head'), parts along dimension 0
There are 2 independent parts, one for each index of `groups`. A program takes and returns all parts, laid end to end along the dimension named above; each array names one. Nothing has to cross between parts.
Inputs may be any that keep to these rules, and one draw needn't show every extreme that they name: `block_mask`: 0 or 1 for each pair of a block of 128 new tokens and a block of 128 history positions of the same session.
All inputs are finite; a program needn't handle non-finite values.
Results may differ from a plain program's by a relative error of at most 0.0013.
Values may be sent and summed in bfloat16 or wider, within the bound.
A program may use at most 64 MiB of HBM per device.

v0:
```python
import functools
import math

import jax
import jax.numpy as jnp
from jax import lax
from jax.experimental import pallas as pl
from jax.experimental.pallas import tpu as pltpu
from jax.sharding import PartitionSpec as P

BLK = 128
NEG = -1e30
TINY = 1e-30
TOP = 32767.0
F32 = jnp.float32
BF16 = jnp.bfloat16


def scores_of(q, k):
    return lax.dot_general(q, k, (((1,), (1,)), ((), ())), preferred_element_type=F32)


def compact(x, eye):
    rows = x.shape[0]
    size = eye.shape[0]
    parts = []
    for at in range(0, rows, size):
        piece = jnp.where(eye, x[at : at + size], 0.0)
        parts.append(jnp.sum(piece, axis=0, keepdims=True)[:, :size])
    return parts[0] if len(parts) == 1 else jnp.concatenate(parts, axis=1)


def eye_of(size):
    return lax.broadcasted_iota(jnp.int32, (size, 128), 0) == lax.broadcasted_iota(
        jnp.int32, (size, 128), 1
    )


def fixed(num):
    big = jnp.maximum(jnp.max(jnp.abs(num), axis=1, keepdims=True), TINY)
    coded = jnp.floor(num * (TOP / big) + 0.5).astype(jnp.int32).astype(jnp.int16)
    return coded, jnp.broadcast_to(big * (1.0 / TOP), num.shape)


def remote(src, dst, send, recv, where):
    return pltpu.make_async_remote_copy(
        src_ref=src,
        dst_ref=dst,
        send_sem=send,
        recv_sem=recv,
        device_id={"ctx": where},
        device_id_type=pl.DeviceIdType.MESH,
    )


def places(n):
    far = n // 2
    me = lax.axis_index("ctx")
    z, y = me // 2, me % 2
    order = sorted(range(1, far), key=lambda d: abs(2 * d - far))
    ahead = [((z + d) % far) * 2 for d in range(far)]
    behind = [((z + far - d) % far) * 2 for d in range(far)]
    return far, me, y, order, ahead, behind


def meet(far, y, ahead):
    barrier = pltpu.get_barrier_semaphore()
    for where in [ahead[d] + y for d in range(1, far)] + [ahead[0] + 1 - y]:
        pl.semaphore_signal(
            barrier, inc=1, device_id={"ctx": where}, device_id_type=pl.DeviceIdType.MESH
        )
    pl.semaphore_wait(barrier, far)


def weights_of(stats):
    tops = stats[0][0:1]
    for st in stats[1:]:
        tops = jnp.maximum(tops, st[0:1])
    total = jnp.zeros_like(tops)
    lines = []
    for st in stats:
        w = jnp.exp2(st[0:1] - tops)
        total = total + st[1:2] * w
        lines.append(st[2:3] * w)
    return tops, total, lines


def fused_kernel(
    n, kv, own, mask_ref, q_ref, k_ref, v_ref, kn_ref, vn_ref, out_ref,
    all_ref, s_ref, p_ref, wide_ref, part_ref, part_st, pair_ref, pair_st, mix_ref, mix_st, line_ref, line_st,
    send_z, recv_z, send_y, recv_y, send_p, recv_p, send_l, recv_l,
):
    far, me, y, order, ahead, behind = places(n)
    rows, hd = q_ref.shape[1:]
    partner = ahead[0] + 1 - y
    z = me // 2
    chunks = BLK // own
    pairs = k_ref.shape[0] // (2 * BLK)
    factor = math.log2(math.e) / math.sqrt(hd)
    eye = eye_of(min(rows, 128))

    meet(far, y, ahead)
    waits = []
    for g in range(kv):
        for d in order:
            waits.append(
                remote(q_ref.at[g], all_ref.at[me, g], send_z.at[d, g], recv_z.at[d, g], ahead[d] + y)
            )
            waits[-1].start()
        waits.append(
            remote(q_ref.at[g], all_ref.at[me, g], send_y.at[0, g], recv_y.at[0, g], partner)
        )
        waits[-1].start()
    all_ref[me] = q_ref[...]

    def relay(g):
        for d in order:
            got = all_ref.at[behind[d] + y, g]
            remote(got, got, send_z.at[d, g], recv_z.at[d, g], ahead[d] + y).wait_recv()
            waits.append(remote(got, got, send_y.at[d, g], recv_y.at[d, g], partner))
            waits[-1].start()

    def arrive(g):
        for d in range(far):
            got = all_ref.at[behind[d] + 1 - y, g]
            remote(got, got, send_y.at[d, g], recv_y.at[d, g], partner).wait_recv()

    def widen(g):
        lanes = slice(g * hd, (g + 1) * hd)
        blank = jnp.zeros((BLK - own, hd), BF16)
        ones = jnp.ones((2 * BLK, hd), BF16)
        fresh = jnp.concatenate([vn_ref[:, lanes], blank], axis=0)
        wide_ref[: 2 * BLK, :hd] = jnp.concatenate([fresh, fresh], axis=0)
        wide_ref[: 2 * BLK, hd:] = ones
        for t in range(pairs):
            v = v_ref[t * 2 * BLK : (t + 1) * 2 * BLK, lanes]
            for copy in range(2):
                at = 2 * BLK * (1 + 2 * t + copy)
                wide_ref[at : at + 2 * BLK, :hd] = v
                wide_ref[at : at + 2 * BLK, hd:] = ones

    def split(at, p):
        cols = p.shape[1]
        hi = p.astype(BF16)
        p_ref[:, at : at + cols] = hi
        p_ref[:, at + cols : at + 2 * cols] = (p - hi.astype(F32)).astype(BF16)

    def attend(both, g):
        q = jnp.concatenate([all_ref[idx, g] for idx in both], axis=0)
        lanes = slice(g * hd, (g + 1) * hd)
        blank = jnp.zeros((BLK - own, hd), BF16)
        col = lax.broadcasted_iota(jnp.int32, (rows, BLK), 1)
        query = lax.broadcasted_iota(jnp.int32, (rows, BLK), 0) // (rows // own)
        s = scores_of(q, jnp.concatenate([kn_ref[:, lanes], blank], axis=0)) * factor
        fresh = jnp.concatenate(
            [
                jnp.where(
                    col <= jnp.minimum(query + (idx - me) * own, own - 1),
                    s[i * rows : (i + 1) * rows],
                    NEG,
                )
                for i, idx in enumerate(both)
            ],
            axis=0,
        )
        top = fresh
        for t in range(pairs):
            s = scores_of(q, k_ref[t * 2 * BLK : (t + 1) * 2 * BLK, lanes]) * factor
            for half in range(2):
                part = s[:, half * BLK : (half + 1) * BLK]
                part = jnp.concatenate(
                    [
                        jnp.where(
                            mask_ref[idx // chunks, 2 * t + half] > 0,
                            part[i * rows : (i + 1) * rows],
                            NEG,
                        )
                        for i, idx in enumerate(both)
                    ],
                    axis=0,
                )
                s_ref[2 * t + half] = part
                top = jnp.maximum(top, part)
        peak = jnp.maximum(jnp.max(top, axis=1, keepdims=True), 0.5 * NEG)
        split(0, jnp.exp2(fresh - peak))
        for t in range(pairs):
            p = jnp.concatenate(
                [jnp.exp2(s_ref[2 * t] - peak), jnp.exp2(s_ref[2 * t + 1] - peak)], axis=1
            )
            split(2 * BLK * (1 + 2 * t), p)
        acc = jnp.dot(p_ref[...], wide_ref[...], preferred_element_type=F32)
        coded, step = fixed(acc[:, :hd])
        peak = jnp.broadcast_to(peak, coded.shape)
        for i, idx in enumerate(both):
            at = slice(i * rows, (i + 1) * rows)
            part_ref[idx, g] = coded[at]
            part_st[idx, g] = jnp.concatenate(
                [
                    compact(peak[at], eye),
                    compact(acc[at, hd:], eye),
                    compact(step[at], eye),
                    jnp.zeros((5, rows), F32),
                ],
                axis=0,
            )

    def to_pair(d, g):
        whose = ahead[d] + 1 - y
        return (
            remote(part_st.at[whose, g], pair_st.at[d, g], send_p.at[d, g, 0], recv_p.at[d, g, 0], partner),
            remote(part_ref.at[whose, g], pair_ref.at[d, g], send_p.at[d, g, 1], recv_p.at[d, g, 1], partner),
        )

    def to_line(d, g):
        whose = ahead[d] + y
        return (
            remote(mix_st.at[d, g], line_st.at[d, g], send_l.at[d, g, 0], recv_l.at[d, g, 0], whose),
            remote(mix_ref.at[d, g], line_ref.at[d, g], send_l.at[d, g, 1], recv_l.at[d, g, 1], whose),
        )

    def merge(g):
        for d in order:
            for copy in to_pair(d, g):
                copy.wait_recv()
            whose = ahead[d] + y
            top, total, lines = weights_of([part_st[whose, g], pair_st[d, g]])
            coded, step = fixed(mixed(lines, [part_ref[whose, g], pair_ref[d, g]]))
            mix_ref[d, g] = coded
            mix_st[d, g] = jnp.concatenate(
                [top, total, compact(step, eye), jnp.zeros((5, rows), F32)], axis=0
            )
        for d in order:
            for copy in to_line(d, g):
                copy.start()
                waits.append(copy)

    def finish(g):
        for copy in to_pair(0, g):
            copy.wait_recv()
        for d in order:
            for copy in to_line(d, g):
                copy.wait_recv()
        _, total, lines = weights_of(
            [part_st[me, g], pair_st[0, g]] + [line_st[d, g] for d in order]
        )
        lines = [line / total for line in lines]
        partials = [part_ref[me, g], pair_ref[0, g]] + [line_ref[d, g] for d in order]
        out_ref[g] = mixed(lines, partials).astype(BF16)

    relay(0)
    for g in range(kv):
        widen(g)
        arrive(g)

        @pl.loop(0, far // 2)
        def _(t):
            attend([lax.rem(z + 2 * t + i, far) * 2 + 1 - y for i in range(2)], g)

        for d in order + [0]:
            for copy in to_pair(d, g):
                copy.start()
                waits.append(copy)
        if g + 1 < kv:
            relay(g + 1)

        @pl.loop(0, far // 2)
        def _(t):
            attend([lax.rem(z + 2 * t + i, far) * 2 + y for i in range(2)], g)

        if g > 0:
            merge(g - 1)
        if g > 1:
            finish(g - 2)
    merge(kv - 1)
    for g in range(max(kv - 2, 0), kv):
        finish(g)
    for copy in waits:
        copy.wait_send()


def per_device(queries, new_keys, new_values, history_keys, history_values, block_mask):
    _, own, heads, hd = queries.shape
    kv = new_keys.shape[2]
    group = heads // kv
    rows = own * group
    context = history_keys.shape[1]
    n = lax.axis_size("ctx")
    far = n // 2

    q = jnp.transpose(queries.reshape(own, kv, group, hd), (1, 0, 2, 3)).reshape(kv, rows, hd)
    vmem = pl.BlockSpec(memory_space=pltpu.VMEM)
    dma = pltpu.SemaphoreType.DMA
    slots = [
        pltpu.VMEM((far, kv, rows, hd), jnp.int16),
        pltpu.VMEM((far, kv, 8, rows), F32),
    ]
    out = pl.pallas_call(
        functools.partial(fused_kernel, n, kv, own),
        in_specs=[pl.BlockSpec(memory_space=pltpu.SMEM)] + [vmem] * 5,
        out_specs=vmem,
        out_shape=jax.ShapeDtypeStruct((kv, rows, hd), BF16),
        scratch_shapes=[
            pltpu.VMEM((n, kv, rows, hd), BF16),
            pltpu.VMEM((context // BLK, 2 * rows, BLK), F32),
            pltpu.VMEM((2 * rows, 2 * (context + BLK)), BF16),
            pltpu.VMEM((2 * (context + BLK), 2 * hd), BF16),
            pltpu.VMEM((n, kv, rows, hd), jnp.int16),
            pltpu.VMEM((n, kv, 8, rows), F32),
        ]
        + slots * 3
        + [dma((far, kv))] * 4
        + [dma((far, kv, 2))] * 4,
        compiler_params=pltpu.CompilerParams(collective_id=0, has_side_effects=True),
        name="fused",
    )(
        block_mask[0],
        q,
        history_keys.reshape(context, kv * hd),
        history_values.reshape(context, kv * hd),
        new_keys.reshape(own, kv * hd),
        new_values.reshape(own, kv * hd),
    )
    out = jnp.transpose(out.reshape(kv, own, group, hd), (1, 0, 2, 3))
    return out.reshape(1, own, heads, hd)


def mixed(lines, partials):
    rows, hd = partials[0].shape
    size = min(rows, 128)
    table = jnp.concatenate(
        lines + [jnp.zeros_like(lines[0])] * (-len(lines) % 8), axis=0
    )
    outs = []
    for at in range(0, rows, size):
        cols = jnp.transpose(table[:, at : at + size])
        total = jnp.zeros((size, hd), F32)
        for i, part in enumerate(partials):
            total = total + cols[:, i : i + 1] * part[at : at + size].astype(jnp.int32).astype(F32)
        outs.append(total)
    return outs[0] if len(outs) == 1 else jnp.concatenate(outs, axis=0)


def solution(mesh):
    spec = P("groups", "ctx", "head", None)
    return jax.shard_map(
        per_device,
        mesh=mesh,
        in_specs=(spec,) * 5 + (P("groups", None, "ctx"),),
        out_specs=spec,
        check_vma=False,
    )
```

profile of v0, /device:TPU:22, one launch (start us, length us, event | category | flops | bytes accessed | tf_op | source)
XLA Modules:
  0.0 89.9 jit_solution(5801567517070155226)
XLA Ops:
  0.0 0.0 copy-start
  0.0 1.4 %copy_bitcast_fusion.4 = (bf16[32,512]{1,0:T(8,128)(2,1)}, bf16[32,512]{1,0:T(8,128)(2,1)}) fusion(bf16[4,8,4,128]{3,2,1,0:T(4,128)(2,1)} %bitcast.33, bf16[4,8,4,128]{3,2,1,0:T(4,128)(2,1)} %bitcast.34), kind=kLoop, calls=%fused_computation.4 | loop fusion | bytes 131072 | tf_op jit(solution)/shard_map/reshape | solution.py:321
  1.5 0.0 copy-done
  1.5 0.7 copy_bitcast_fusion.3.q_ref
  2.2 3.2 %copy_bitcast_fusion = (bf16[1024,512]{1,0:T(8,128)(2,1)}, bf16[1024,512]{1,0:T(8,128)(2,1)}) fusion(bf16[128,8,4,128]{3,2,1,0:T(4,128)(2,1)} %bitcast.31, bf16[128,8,4,128]{3,2,1,0:T(4,128)(2,1)} %bitcast.32), kind=kLoop, calls=%fused_computation | loop fusion | bytes 4194304 | tf_op jit(solution)/shard_map/reshape | solution.py:319
  5.4 82.7 %fused.1 = bf16[4,256,128]{2,1,0:T(8,128)(2,1)} custom-call(s32[2,8]{1,0:T(2,128)} %bitcast.35, bf16[4,256,128]{2,1,0:T(8,128)(2,1)} %copy_bitcast_fusion.3.q_ref, bf16[1024,512]{1,0:T(8,128)(2,1)} %get-tuple-element.6.k_ref, bf16[1024,512]{1,0:T(8,128)(2,1)} %get-tuple-element.5.v_ref, bf16[32,512]{1,0:T(8,128)(2,1)} %get-tuple-element.8.kn_ref, ...), custom_call_target="tpu_custom_call" | custom-call | tf_op jit(solution)/shard_map/fused/pallas_call | solution.py:297
  88.2 1.7 %copy_bitcast_fusion.2 = bf16[1,32,32,128]{3,2,1,0:T(8,128)(2,1)} fusion(bf16[4,256,128]{2,1,0:T(8,128)(2,1)} %fused.1), kind=kLoop, calls=%fused_computation.2 | loop fusion | bytes 524288 | tf_op jit(solution)/shard_map/reshape | solution.py:324
Async XLA Ops:
  0.0 1.5 %copy-start = (bf16[1,32,32,128]{3,2,1,0:T(8,128)(2,1)S(1)}, bf16[1,32,32,128]{3,2,1,0:T(8,128)(2,1)}, u32[]{:S(2)}) copy-start(bf16[1,32,32,128]{3,2,1,0:T(8,128)(2,1)} %param.6) | copy-start | bytes 786436
where the time goes:
time: 90.1 us; the launch traced here: 89.9 us
  Pallas kernels  82.7 us (92%)
  local copies, waits for them, and re-layouts  7.12 us (8%)
    pallas_call x1, Pallas kernels, per_device(): pl.pallas_call(functools.partial(fused_kernel, n, kv, own), in_specs=[pl....  82.7 us
    reshape x1, local copies, waits for them, and re-layouts, per_device(): history_values.reshape(context, kv * hd)  3.22 us

commit v1 on v0

v1 whole, which is shorter than its diff:
```python
import functools
import math

import jax
import jax.numpy as jnp
from jax import lax
from jax.experimental import pallas as pl
from jax.experimental.pallas import tpu as pltpu
from jax.sharding import PartitionSpec as P

BLK = 128
NEG = -1e30
TINY = 1e-30
TOP = 32767.0
F32 = jnp.float32
BF16 = jnp.bfloat16
I16 = jnp.int16


def scores_of(q, k):
    return lax.dot_general(q, k, (((1,), (1,)), ((), ())), preferred_element_type=F32)


def xor(a, b, size):
    total, bit = 0, 1
    while bit < size:
        total = total + bit * ((a // bit + b // bit) % 2)
        bit *= 2
    return total


def remote(src, dst, send, recv, where):
    return pltpu.make_async_remote_copy(
        src_ref=src,
        dst_ref=dst,
        send_sem=send,
        recv_sem=recv,
        device_id={"ctx": where},
        device_id_type=pl.DeviceIdType.MESH,
    )


def compact(x, eye):
    return jnp.sum(jnp.where(eye, x, 0.0), axis=0, keepdims=True)


def fused_kernel(
    n, kv, own, mask_ref, q_ref, k_ref, v_ref, kn_ref, vn_ref, out_ref,
    allq_ref, kraw_ref, vraw_ref, nk_ref, nv_ref, bias_ref, kk_ref, wv_ref, kkn_ref, wvn_ref,
    s_ref, sn_ref, p_ref, pn_ref, acc_ref, den_ref, peak_ref,
    part_ref, part_st, pair_ref, pair_st, far_ref, far_st, mine_ref, got_ref,
    send_q, recv_q, send_r, recv_r, send_y, recv_y, send_k, recv_k, send_n, recv_n,
    send_p, recv_p, send_f, recv_f, send_o, recv_o,
):
    far, half = n // 2, kv // 2
    me = lax.axis_index("ctx")
    z, y = me // 2, me % 2
    partner = z * 2 + 1 - y
    rows, hd = q_ref.shape[1:]
    context = k_ref.shape[0]
    blocks = context // BLK
    both = 2 * rows
    span = min(256, both)
    group = rows // own
    factor = math.log2(math.e) / math.sqrt(hd)
    eye = lax.broadcasted_iota(jnp.int32, (128, 128), 0) == lax.broadcasted_iota(
        jnp.int32, (128, 128), 1
    )
    direct = ([1] if far > 1 else []) + list(range(2, far, 2))

    def plane(d):
        return xor(z, d, far)

    def device(d):
        return plane(d) * 2 + y

    def part_of(which):
        return pl.ds(pl.multiple_of(which * rows, rows), rows)

    def lanes_of(head, count):
        return pl.ds(pl.multiple_of(head * hd, hd), count * hd)

    barrier = pltpu.get_barrier_semaphore()
    for where in [device(d) for d in direct] + [partner]:
        pl.semaphore_signal(
            barrier, inc=1, device_id={"ctx": where}, device_id_type=pl.DeviceIdType.MESH
        )
    for t in range(2):
        for b in range(blocks):
            bias_ref[0, t, b : b + 1, :] = jnp.full(
                (1, 128), jnp.where(mask_ref[t, b] > 0, 0.0, NEG), F32
            )
    pl.semaphore_wait(barrier, len(direct) + 1)

    def swap_q(i):
        return remote(
            q_ref.at[(1 - y) * half + i], allq_ref.at[z, i, part_of(y)], send_y.at[i], recv_y.at[i], partner
        )

    def got_q(i):
        return remote(
            q_ref.at[i], allq_ref.at[z, i, part_of(1 - y)], send_y.at[i], recv_y.at[i], partner
        )

    def mine_to(i, d):
        return remote(
            q_ref.at[y * half + i], allq_ref.at[z, i, part_of(y)], send_q.at[i, d, 0], recv_q.at[i, d, 0], device(d)
        )

    def theirs_to(i, d):
        src = allq_ref.at[z, i, part_of(1 - y)]
        return remote(src, src, send_q.at[i, d, 1], recv_q.at[i, d, 1], device(d))

    def plane_from(i, d):
        return [
            remote(
                q_ref.at[i], allq_ref.at[plane(d), i, part_of(which)],
                send_q.at[i, d, at], recv_q.at[i, d, at], device(d),
            )
            for at, which in ((0, y), (1, 1 - y))
        ]

    def relay(i, d):
        src = allq_ref.at[plane(d), i]
        return remote(src, src, send_r.at[i, d], recv_r.at[i, d], device(1))

    def relayed(i, d):
        src = allq_ref.at[plane(d), i]
        return remote(src, src, send_r.at[i, d - 1], recv_r.at[i, d - 1], device(1))

    def swap_kv(i):
        lanes = lanes_of((1 - y) * half + i, 1)
        return [
            remote(k_ref.at[:, lanes], kraw_ref.at[i], send_k.at[i, 0], recv_k.at[i, 0], partner),
            remote(v_ref.at[:, lanes], vraw_ref.at[i], send_k.at[i, 1], recv_k.at[i, 1], partner),
        ]

    lanes = lanes_of((1 - y) * half, half)
    fresh = [
        remote(kn_ref.at[:, lanes], nk_ref, send_n.at[0], recv_n.at[0], partner),
        remote(vn_ref.at[:, lanes], nv_ref, send_n.at[1], recv_n.at[1], partner),
        remote(bias_ref.at[0], bias_ref.at[1], send_n.at[2], recv_n.at[2], partner),
    ]
    swap_q(0).start()
    for copy in fresh[:2]:
        copy.start()
    for i in range(1, half):
        swap_q(i).start()
    fresh[2].start()
    for i in range(half):
        for copy in swap_kv(i):
            copy.start()
    for i in range(half):
        for d in direct:
            mine_to(i, d).start()

    ones = jnp.ones((context, hd), BF16)
    for i in range(half):
        allq_ref[z, i, part_of(y)] = q_ref[y * half + i]
        lane = lanes_of(y * half + i, 1)
        k = k_ref[:, lane]
        kk_ref[i, 0, :, :hd] = k
        kk_ref[i, 0, :, hd:] = k
        wv_ref[i, 0, :, :hd] = v_ref[:, lane]
        for side in range(2):
            wv_ref[i, side, :, hd:] = ones

    def spread(i):
        swap_done = got_q(i)
        swap_done.wait_recv()
        for d in direct:
            theirs_to(i, d).start()

    spread(0)
    for copy in fresh[:2]:
        copy.wait_recv()
    blank = jnp.zeros((BLK - 2 * own, hd), BF16)
    for i in range(half):
        lane, here = lanes_of(y * half + i, 1), slice(i * hd, (i + 1) * hd)
        for mine, theirs, at in ((kn_ref[:, lane], nk_ref[:, here], 0), (vn_ref[:, lane], nv_ref[:, here], 1)):
            first = jnp.where(y == 0, mine, theirs)
            second = jnp.where(y == 0, theirs, mine)
            tile = jnp.concatenate([first, second, blank], axis=0)
            if at == 0:
                kkn_ref[i] = jnp.concatenate([tile, tile], axis=1)
            else:
                wide = jnp.concatenate([tile, jnp.ones_like(tile)], axis=1)
                wvn_ref[i] = jnp.concatenate([wide, wide], axis=0)

    def attend(i, p, side):
        qb = p * 2 * own // BLK
        for c in range(both // span):
            at = slice(c * span, (c + 1) * span)
            slot = c % 2
            q = allq_ref[p, i, at].astype(F32) * factor
            hi = q.astype(BF16)
            q = jnp.concatenate([hi, (q - hi.astype(F32)).astype(BF16)], axis=1)
            if side == 0:
                col = lax.broadcasted_iota(jnp.int32, (span, BLK), 1)
                token = (lax.broadcasted_iota(jnp.int32, (span, BLK), 0) + c * span) // group
                seen = col <= jnp.minimum(token + (p - z) * 2 * own, 2 * own - 1)
                top = jnp.where(seen, scores_of(q, kkn_ref[i]), NEG)
                sn_ref[slot] = top
            else:
                top = peak_ref[i, p, at]
            for t in range(blocks // 2):
                s = scores_of(q, kk_ref[i, side, t * 2 * BLK : (t + 1) * 2 * BLK])
                for h in range(2):
                    b = 2 * t + h
                    part = s[:, h * BLK : (h + 1) * BLK] + bias_ref[side, qb, b : b + 1, :]
                    s_ref[slot, b] = part
                    top = jnp.maximum(top, part)
            peak = jnp.maximum(jnp.max(top, axis=1, keepdims=True), 0.5 * NEG)
            for b in range(blocks):
                w = jnp.exp2(s_ref[slot, b] - peak)
                hi = w.astype(BF16)
                here = slice(b * BLK, (b + 1) * BLK)
                p_ref[slot, :span, here] = hi
                p_ref[slot, span:, here] = (w - hi.astype(F32)).astype(BF16)
            acc = jnp.dot(p_ref[slot], wv_ref[i, side], preferred_element_type=F32)
            acc = acc[:span] + acc[span:]
            if side == 0:
                w = jnp.exp2(sn_ref[slot] - peak)
                hi = w.astype(BF16)
                pn_ref[slot, :, :BLK] = hi
                pn_ref[slot, :, BLK:] = (w - hi.astype(F32)).astype(BF16)
                acc = acc + jnp.dot(pn_ref[slot], wvn_ref[i], preferred_element_type=F32)
                num, den = acc[:, :hd], acc[:, hd:]
            else:
                old = jnp.exp2(peak_ref[i, p, at] - peak)
                num = acc[:, :hd] + acc_ref[i, p, at] * old
                den = acc[:, hd:] + den_ref[i, p, at] * old
            acc_ref[i, p, at] = num
            den_ref[i, p, at] = den
            peak_ref[i, p, at] = jnp.broadcast_to(peak, (span, hd))

    chunks = both // 128

    def encode(i, p, d):
        lines = []
        for c in range(chunks):
            at = slice(c * 128, (c + 1) * 128)
            num = acc_ref[i, p, at]
            big = jnp.maximum(jnp.max(jnp.abs(num), axis=1, keepdims=True), TINY)
            part_ref[i, d, at] = jnp.floor(num * (TOP / big) + 0.5).astype(jnp.int32).astype(I16)
            lines += [
                compact(peak_ref[i, p, at], eye),
                compact(den_ref[i, p, at], eye),
                compact(jnp.broadcast_to(big * (1.0 / TOP), (128, 128)), eye),
            ]
        short = part_st.shape[2] - len(lines)
        part_st[i, d] = jnp.concatenate(lines + [jnp.zeros((short, 128), F32)], axis=0)

    def absorb(i, p, codes, stats):
        for c in range(chunks):
            at = slice(c * 128, (c + 1) * 128)
            table = jnp.concatenate([stats[3 * c : 3 * c + 3], jnp.zeros((5, 128), F32)], axis=0)
            cols = jnp.transpose(table)
            mine, theirs = peak_ref[i, p, at], cols[:, 0:1]
            peak = jnp.maximum(mine, theirs)
            old, new = jnp.exp2(mine - peak), jnp.exp2(theirs - peak)
            coded = codes[at].astype(jnp.int32).astype(F32)
            acc_ref[i, p, at] = acc_ref[i, p, at] * old + coded * (cols[:, 2:3] * new)
            den_ref[i, p, at] = den_ref[i, p, at] * old + cols[:, 1:2] * new
            peak_ref[i, p, at] = peak

    def to_pair(i, d):
        e = d // 2
        return [
            remote(part_st.at[i, d], pair_st.at[i, e], send_p.at[i, e, 0], recv_p.at[i, e, 0], device(1)),
            remote(part_ref.at[i, d], pair_ref.at[i, e], send_p.at[i, e, 1], recv_p.at[i, e, 1], device(1)),
        ]

    def to_far(i, d):
        e = d // 2
        return [
            remote(part_st.at[i, d], far_st.at[i, e], send_f.at[i, e, 0], recv_f.at[i, e, 0], device(d)),
            remote(part_ref.at[i, d], far_ref.at[i, e], send_f.at[i, e, 1], recv_f.at[i, e, 1], device(d)),
        ]

    def to_out(i):
        return remote(mine_ref.at[i], got_ref.at[i], send_o.at[i], recv_o.at[i], partner)

    def first(i, lo, hi):
        @pl.loop(lo, hi)
        def _(d):
            straight = jnp.logical_or(d % 2 == 0, d == 1)

            @pl.when(straight)
            def _():
                for copy in plane_from(i, d):
                    copy.wait_recv()

            @pl.when(d % 2 == 0)
            def _():
                relay(i, d).start()

            @pl.when(jnp.logical_not(straight))
            def _():
                relayed(i, d).wait_recv()

            attend(i, plane(d), 0)

    def odd(i):
        @pl.loop(0, far // 2)
        def _(t):
            d = far - 1 - 2 * t
            attend(i, plane(d), 1)
            encode(i, plane(d), d)
            for copy in to_pair(i, d):
                copy.start()

    def even(i):
        @pl.loop(0, far // 2 - 1)
        def _(t):
            d = far - 2 - 2 * t
            attend(i, plane(d), 1)
            for copy in to_pair(i, d):
                copy.wait_recv()
            absorb(i, plane(d), pair_ref.at[i, d // 2], pair_st.at[i, d // 2])
            encode(i, plane(d), d)
            for copy in to_far(i, d):
                copy.start()

    def finish(i):
        if far > 1:
            for copy in to_pair(i, 0):
                copy.wait_recv()
            absorb(i, z, pair_ref.at[i, 0], pair_st.at[i, 0])
        for d in range(2, far, 2):
            for copy in to_far(i, d):
                copy.wait_recv()
            absorb(i, z, far_ref.at[i, d // 2], far_st.at[i, d // 2])
        here = part_of(1 - y)
        mine_ref[i] = (acc_ref[i, z, here] / den_ref[i, z, here]).astype(BF16)
        to_out(i).start()
        here = part_of(y)
        out_ref[y * half + i] = (acc_ref[i, z, here] / den_ref[i, z, here]).astype(BF16)

    def widen(i):
        for copy in swap_kv(i):
            copy.wait_recv()
        kk_ref[i, 1, :, :hd] = kraw_ref[i]
        kk_ref[i, 1, :, hd:] = kraw_ref[i]
        wv_ref[i, 1, :, :hd] = vraw_ref[i]

    attend(0, z, 0)
    for i in range(1, half):
        spread(i)
    first(0, 1, far)
    fresh[2].wait_recv()
    for i in range(half):
        widen(i)
        if i + 1 == half and i > 0:
            odd(i)
            attend(i, z, 1)
            finish(i - 1)
            even(i)
            finish(i)
        else:
            odd(i)
            attend(i, z, 1)
            if i > 0:
                finish(i - 1)
            if i + 1 < half:
                attend(i + 1, z, 0)
                first(i + 1, 1, far)
            even(i)
            if half == 1:
                finish(i)
    for i in range(half):
        to_out(i).wait_recv()
        out_ref[(1 - y) * half + i] = got_ref[i]

    for copy in fresh:
        copy.wait_send()
    for i in range(half):
        swap_q(i).wait_send()
        to_out(i).wait_send()
        for copy in swap_kv(i):
            copy.wait_send()
        for d in direct:
            mine_to(i, d).wait_send()
            theirs_to(i, d).wait_send()
        for d in range(2, far, 2):
            relay(i, d).wait_send()
            for copy in to_far(i, d):
                copy.wait_send()
        for d in range(1, far, 2):
            for copy in to_pair(i, d):
                copy.wait_send()


def per_device(queries, new_keys, new_values, history_keys, history_values, block_mask):
    _, own, heads, hd = queries.shape
    kv = new_keys.shape[2]
    group = heads // kv
    rows = own * group
    context = history_keys.shape[1]
    blocks = context // BLK
    n = lax.axis_size("ctx")
    far, half = n // 2, kv // 2
    both = 2 * rows
    span = min(256, both)
    lines = -(-3 * (both // 128) // 8) * 8

    q = jnp.transpose(queries.reshape(own, kv, group, hd), (1, 0, 2, 3)).reshape(kv, rows, hd)
    vmem = pl.BlockSpec(memory_space=pltpu.VMEM)
    dma = pltpu.SemaphoreType.DMA
    slots = [
        pltpu.VMEM((half, far // 2, both, hd), I16),
        pltpu.VMEM((half, far // 2, lines, 128), F32),
    ]
    out = pl.pallas_call(
        functools.partial(fused_kernel, n, kv, own),
        in_specs=[pl.BlockSpec(memory_space=pltpu.SMEM)] + [vmem] * 5,
        out_specs=vmem,
        out_shape=jax.ShapeDtypeStruct((kv, rows, hd), BF16),
        scratch_shapes=[
            pltpu.VMEM((far, half, both, hd), BF16),
            pltpu.VMEM((half, context, hd), BF16),
            pltpu.VMEM((half, context, hd), BF16),
            pltpu.VMEM((own, half * hd), BF16),
            pltpu.VMEM((own, half * hd), BF16),
            pltpu.VMEM((2, 2, blocks, 128), F32),
            pltpu.VMEM((half, 2, context, 2 * hd), BF16),
            pltpu.VMEM((half, 2, context, 2 * hd), BF16),
            pltpu.VMEM((half, BLK, 2 * hd), BF16),
            pltpu.VMEM((half, 2 * BLK, 2 * hd), BF16),
            pltpu.VMEM((2, blocks, span, BLK), F32),
            pltpu.VMEM((2, span, BLK), F32),
            pltpu.VMEM((2, 2 * span, context), BF16),
            pltpu.VMEM((2, span, 2 * BLK), BF16),
            pltpu.VMEM((half, far, both, hd), F32),
            pltpu.VMEM((half, far, both, hd), F32),
            pltpu.VMEM((half, far, both, hd), F32),
            pltpu.VMEM((half, far, both, hd), I16),
            pltpu.VMEM((half, far, lines, 128), F32),
        ]
        + slots * 2
        + [
            pltpu.VMEM((half, rows, hd), BF16),
            pltpu.VMEM((half, rows, hd), BF16),
        ]
        + [dma((half, far, 2))] * 2
        + [dma((half, far))] * 2
        + [dma((half,))] * 2
        + [dma((half, 2))] * 2
        + [dma((3,))] * 2
        + [dma((half, far // 2, 2))] * 4
        + [dma((half,))] * 2,
        compiler_params=pltpu.CompilerParams(collective_id=0, has_side_effects=True),
        name="fused",
    )(
        block_mask[0],
        q,
        history_keys.reshape(context, kv * hd),
        history_values.reshape(context, kv * hd),
        new_keys.reshape(own, kv * hd),
        new_values.reshape(own, kv * hd),
    )
    out = jnp.transpose(out.reshape(kv, own, group, hd), (1, 0, 2, 3))
    return out.reshape(1, own, heads, hd)


def solution(mesh):
    spec = P("groups", "ctx", "head", None)
    return jax.shard_map(
        per_device,
        mesh=mesh,
        in_specs=(spec,) * 5 + (P("groups", None, "ctx"),),
        out_specs=spec,
        check_vma=False,
    )
```

time: 90.1 us -> 68.8 us (0.76)
  the two profiles are of different devices: /device:TPU:22 before, /device:TPU:0 now
where the time goes in v1:
time: 68.8 us; the launch traced here: 68.6 us
  Pallas kernels  61.5 us (89%)
  local copies, waits for them, and re-layouts  7.12 us (10%)
    pallas_call x1, Pallas kernels, per_device(): pl.pallas_call(functools.partial(fused_kernel, n, kv, own), in_specs=[pl....  61.5 us
    reshape x1, local copies, waits for them, and re-layouts, per_device(): history_values.reshape(context, kv * hd)  3.22 us
    reshape x1, local copies, waits for them, and re-layouts, per_device(): return out.reshape(1, own, heads, hd)  1.7 us
    reshape x1, local copies, waits for them, and re-layouts, per_device(): new_values.reshape(own, kv * hd)  1.45 us

profile of v1, /device:TPU:0, one launch (start us, length us, event | category | flops | bytes accessed | tf_op | source)
XLA Modules:
  0.0 68.6 jit_solution(11673828765588758126)
XLA Ops:
  0.0 0.0 copy-start
  0.0 1.4 %copy_bitcast_fusion.4 = (bf16[32,512]{1,0:T(8,128)(2,1)}, bf16[32,512]{1,0:T(8,128)(2,1)}) fusion(bf16[4,8,4,128]{3,2,1,0:T(4,128)(2,1)} %bitcast.33, bf16[4,8,4,128]{3,2,1,0:T(4,128)(2,1)} %bitcast.34), kind=kLoop, calls=%fused_computation.4 | loop fusion | bytes 131072 | tf_op jit(solution)/shard_map/reshape | solution.py:460
  1.5 0.0 copy-done
  1.5 0.7 %copy_bitcast_fusion.3.q_ref = bf16[4,256,128]{2,1,0:T(8,128)(2,1)} fusion(bf16[1,32,32,128]{3,2,1,0:T(8,128)(2,1)S(1)} %copy-done), kind=kLoop, calls=%fused_computation.3 | loop fusion | bytes 524288 | tf_op jit(solution)/shard_map/reshape | solution.py:407
  2.2 3.2 %copy_bitcast_fusion = (bf16[1024,512]{1,0:T(8,128)(2,1)}, bf16[1024,512]{1,0:T(8,128)(2,1)}) fusion(bf16[128,8,4,128]{3,2,1,0:T(4,128)(2,1)} %bitcast.31, bf16[128,8,4,128]{3,2,1,0:T(4,128)(2,1)} %bitcast.32), kind=kLoop, calls=%fused_computation | loop fusion | bytes 4194304 | tf_op jit(solution)/shard_map/reshape | solution.py:458
  5.4 61.5 %fused.1 = bf16[4,256,128]{2,1,0:T(8,128)(2,1)} custom-call(s32[2,8]{1,0:T(2,128)} %bitcast.35, bf16[4,256,128]{2,1,0:T(8,128)(2,1)} %copy_bitcast_fusion.3.q_ref, bf16[1024,512]{1,0:T(8,128)(2,1)} %get-tuple-element.6.k_ref, bf16[1024,512]{1,0:T(8,128)(2,1)} %get-tuple-element.5.v_ref, bf16[32,512]{1,0:T(8,128)(2,1)} %get-tuple-element.8.kn_ref, ...), custom_call_target="tpu_custom_call" | custom-call | tf_op jit(solution)/shard_map/fused/pallas_call | solution.py:414
  66.9 1.7 %copy_bitcast_fusion.2 = bf16[1,32,32,128]{3,2,1,0:T(8,128)(2,1)} fusion(bf16[4,256,128]{2,1,0:T(8,128)(2,1)} %fused.1), kind=kLoop, calls=%fused_computation.2 | loop fusion | bytes 524288 | tf_op jit(solution)/shard_map/reshape | solution.py:463
Async XLA Ops:
  0.0 1.5 %copy-start = (bf16[1,32,32,128]{3,2,1,0:T(8,128)(2,1)S(1)}, bf16[1,32,32,128]{3,2,1,0:T(8,128)(2,1)}, u32[]{:S(2)}) copy-start(bf16[1,32,32,128]{3,2,1,0:T(8,128)(2,1)} %param.6) | copy-start | bytes 786436

commit v2 on v1

--- a/solution.py
+++ b/solution.py
@@ -46,7 +46,7 @@
 
 def fused_kernel(
     n, kv, own, mask_ref, q_ref, k_ref, v_ref, kn_ref, vn_ref, out_ref,
-    allq_ref, kraw_ref, vraw_ref, nk_ref, nv_ref, bias_ref, kk_ref, wv_ref, kkn_ref, wvn_ref,
+    kd_ref, vd_ref, nd_ref, allq_ref, kraw_ref, vraw_ref, nk_ref, nv_ref, bias_ref, kk_ref, wv_ref, kkn_ref, wvn_ref,
     s_ref, sn_ref, p_ref, pn_ref, acc_ref, den_ref, peak_ref,
     part_ref, part_st, pair_ref, pair_st, far_ref, far_st, mine_ref, got_ref,
     send_q, recv_q, send_r, recv_r, send_y, recv_y, send_k, recv_k, send_n, recv_n,
@@ -57,7 +57,7 @@
     z, y = me // 2, me % 2
     partner = z * 2 + 1 - y
     rows, hd = q_ref.shape[1:]
-    context = k_ref.shape[0]
+    context = kraw_ref.shape[1]
     blocks = context // BLK
     both = 2 * rows
     span = min(256, both)
@@ -76,9 +76,6 @@
 
     def part_of(which):
         return pl.ds(pl.multiple_of(which * rows, rows), rows)
-
-    def lanes_of(head, count):
-        return pl.ds(pl.multiple_of(head * hd, hd), count * hd)
 
     barrier = pltpu.get_barrier_semaphore()
     for where in [device(d) for d in direct] + [partner]:
@@ -129,39 +126,57 @@
         return remote(src, src, send_r.at[i, d - 1], recv_r.at[i, d - 1], device(1))
 
     def swap_kv(i):
-        lanes = lanes_of((1 - y) * half + i, 1)
+        head = (1 - y) * half + i
         return [
-            remote(k_ref.at[:, lanes], kraw_ref.at[i], send_k.at[i, 0], recv_k.at[i, 0], partner),
-            remote(v_ref.at[:, lanes], vraw_ref.at[i], send_k.at[i, 1], recv_k.at[i, 1], partner),
-        ]
-
-    lanes = lanes_of((1 - y) * half, half)
+            remote(kd_ref.at[head], kraw_ref.at[i], send_k.at[i, 0], recv_k.at[i, 0], partner),
+            remote(vd_ref.at[head], vraw_ref.at[i], send_k.at[i, 1], recv_k.at[i, 1], partner),
+        ]
+
+    def sorter(size):
+        to = lax.broadcasted_iota(jnp.int32, (size, size), 0)
+        at = lax.broadcasted_iota(jnp.int32, (size, size), 1)
+        per = size // kv
+        return jnp.where(at == (to % per) * kv + to // per, 1.0, 0.0).astype(BF16)
+
+    def sort_heads(src, dst, order):
+        size = order.shape[0]
+        per = size // kv
+        for t in range(src.shape[0] // size):
+            got = jnp.dot(order, src[t * size : (t + 1) * size], preferred_element_type=F32).astype(BF16)
+            for h in range(kv):
+                dst[h, t * per : (t + 1) * per] = got[h * per : (h + 1) * per]
+
+    theirs = pl.ds((1 - y) * half, half)
     fresh = [
-        remote(kn_ref.at[:, lanes], nk_ref, send_n.at[0], recv_n.at[0], partner),
-        remote(vn_ref.at[:, lanes], nv_ref, send_n.at[1], recv_n.at[1], partner),
+        remote(nd_ref.at[0, theirs], nk_ref, send_n.at[0], recv_n.at[0], partner),
+        remote(nd_ref.at[1, theirs], nv_ref, send_n.at[1], recv_n.at[1], partner),
         remote(bias_ref.at[0], bias_ref.at[1], send_n.at[2], recv_n.at[2], partner),
     ]
-    swap_q(0).start()
-    for copy in fresh[:2]:
+    for i in range(half):
+        swap_q(i).start()
+        for d in direct:
+            mine_to(i, d).start()
+    order = sorter(2 * BLK)
+    sort_heads(k_ref, kd_ref, order)
+    swap_kv(0)[0].start()
+    sort_heads(v_ref, vd_ref, order)
+    order = sorter(kn_ref.shape[0])
+    sort_heads(kn_ref, nd_ref.at[0], order)
+    sort_heads(vn_ref, nd_ref.at[1], order)
+    for copy in fresh:
         copy.start()
+    swap_kv(0)[1].start()
     for i in range(1, half):
-        swap_q(i).start()
-    fresh[2].start()
-    for i in range(half):
         for copy in swap_kv(i):
             copy.start()
-    for i in range(half):
-        for d in direct:
-            mine_to(i, d).start()
 
     ones = jnp.ones((context, hd), BF16)
     for i in range(half):
         allq_ref[z, i, part_of(y)] = q_ref[y * half + i]
-        lane = lanes_of(y * half + i, 1)
-        k = k_ref[:, lane]
+        k = kd_ref[y * half + i]
         kk_ref[i, 0, :, :hd] = k
         kk_ref[i, 0, :, hd:] = k
-        wv_ref[i, 0, :, :hd] = v_ref[:, lane]
+        wv_ref[i, 0, :, :hd] = vd_ref[y * half + i]
         for side in range(2):
             wv_ref[i, side, :, hd:] = ones
 
@@ -176,10 +191,10 @@
         copy.wait_recv()
     blank = jnp.zeros((BLK - 2 * own, hd), BF16)
     for i in range(half):
-        lane, here = lanes_of(y * half + i, 1), slice(i * hd, (i + 1) * hd)
-        for mine, theirs, at in ((kn_ref[:, lane], nk_ref[:, here], 0), (vn_ref[:, lane], nv_ref[:, here], 1)):
-            first = jnp.where(y == 0, mine, theirs)
-            second = jnp.where(y == 0, theirs, mine)
+        for at, got in ((0, nk_ref[i]), (1, nv_ref[i])):
+            mine = nd_ref[at, y * half + i]
+            first = jnp.where(y == 0, mine, got)
+            second = jnp.where(y == 0, got, mine)
             tile = jnp.concatenate([first, second, blank], axis=0)
             if at == 0:
                 kkn_ref[i] = jnp.concatenate([tile, tile], axis=1)
@@ -417,11 +432,14 @@
         out_specs=vmem,
         out_shape=jax.ShapeDtypeStruct((kv, rows, hd), BF16),
         scratch_shapes=[
+            pltpu.VMEM((kv, context, hd), BF16),
+            pltpu.VMEM((kv, context, hd), BF16),
+            pltpu.VMEM((2, kv, own, hd), BF16),
             pltpu.VMEM((far, half, both, hd), BF16),
             pltpu.VMEM((half, context, hd), BF16),
             pltpu.VMEM((half, context, hd), BF16),
-            pltpu.VMEM((own, half * hd), BF16),
-            pltpu.VMEM((own, half * hd), BF16),
+            pltpu.VMEM((half, own, hd), BF16),
+            pltpu.VMEM((half, own, hd), BF16),
             pltpu.VMEM((2, 2, blocks, 128), F32),
             pltpu.VMEM((half, 2, context, 2 * hd), BF16),
             pltpu.VMEM((half, 2, context, 2 * hd), BF16),
@@ -454,10 +472,10 @@
     )(
         block_mask[0],
         q,
-        history_keys.reshape(context, kv * hd),
-        history_values.reshape(context, kv * hd),
-        new_keys.reshape(own, kv * hd),
-        new_values.reshape(own, kv * hd),
+        history_keys.reshape(context * kv, hd),
+        history_values.reshape(context * kv, hd),
+        new_keys.reshape(own * kv, hd),
+        new_values.reshape(own * kv, hd),
     )
     out = jnp.transpose(out.reshape(kv, own, group, hd), (1, 0, 2, 3))
     return out.reshape(1, own, heads, hd)

time: 68.8 us -> 63.2 us (0.919)
  local copies, waits for them, and re-layouts: 7.12 us -> 3.4 us
  Pallas kernels: 61.5 us -> 59.6 us
    reshape x2 -> x0, local copies, waits for them, and re-layouts: 4.67 us -> none  [the longest x1 3.22 us: per_device(): history_values.reshape(context, kv * hd)]
    pallas_call x1, Pallas kernels: 61.5 us -> 59.6 us  [per_device(): pl.pallas_call(functools.partial(fused_kernel, n, kv, own), in_specs=[pl....]
    unnamed x2, local copies, waits for them, and re-layouts: 0.01 us -> 0.95 us
where the time goes in v2:
time: 63.2 us; the launch traced here: 63 us
  Pallas kernels  59.6 us (94%)
  local copies, waits for them, and re-layouts  3.4 us (5%)
    pallas_call x1, Pallas kernels, per_device(): pl.pallas_call(functools.partial(fused_kernel, n, kv, own), in_specs=[pl....  59.6 us
    reshape x1, local copies, waits for them, and re-layouts, per_device(): return out.reshape(1, own, heads, hd)  1.7 us

profile of v2, /device:TPU:0, one launch (start us, length us, event | category | flops | bytes accessed | tf_op | source)
XLA Modules:
  0.0 63.0 jit_solution(6174140587497270573)
XLA Ops:
  0.0 0.0 copy-start
  0.0 0.9 %copy-done = bf16[1,32,32,128]{3,2,1,0:T(8,128)(2,1)S(1)} copy-done((bf16[1,32,32,128]{3,2,1,0:T(8,128)(2,1)S(1)}, bf16[1,32,32,128]{3,2,1,0:T(8,128)(2,1)}, u32[]{:S(2)}) %copy-start) | copy-done | bytes 262168
  1.0 0.7 %copy_bitcast_fusion.1.q_ref = bf16[4,256,128]{2,1,0:T(8,128)(2,1)} fusion(bf16[1,32,32,128]{3,2,1,0:T(8,128)(2,1)S(1)} %copy-done), kind=kLoop, calls=%fused_computation.1 | loop fusion | bytes 524288 | tf_op jit(solution)/shard_map/reshape | solution.py:422
  1.7 59.6 %fused.1 = bf16[4,256,128]{2,1,0:T(8,128)(2,1)} custom-call(s32[2,8]{1,0:T(2,128)} %bitcast.23, bf16[4,256,128]{2,1,0:T(8,128)(2,1)} %copy_bitcast_fusion.1.q_ref, bf16[4096,128]{1,0:T(8,128)(2,1)} %bitcast.19, bf16[4096,128]{1,0:T(8,128)(2,1)} %bitcast.20, bf16[128,128]{1,0:T(8,128)(2,1)} %bitcast.21, bf16[128,128]{1,0:T(8,128)(2,1)} %bitcast.22), custom_call_target="tpu_custom_call" | custom-call | tf_op jit(solution)/shard_map/fused/pallas_call | solution.py:429
  61.3 1.7 %copy_bitcast_fusion = bf16[1,32,32,128]{3,2,1,0:T(8,128)(2,1)} fusion(bf16[4,256,128]{2,1,0:T(8,128)(2,1)} %fused.1), kind=kLoop, calls=%fused_computation | loop fusion | bytes 524288 | tf_op jit(solution)/shard_map/reshape | solution.py:481
Async XLA Ops:
  0.0 1.0 %copy-start = (bf16[1,32,32,128]{3,2,1,0:T(8,128)(2,1)S(1)}, bf16[1,32,32,128]{3,2,1,0:T(8,128)(2,1)}, u32[]{:S(2)}) copy-start(bf16[1,32,32,128]{3,2,1,0:T(8,128)(2,1)} %param.6) | copy-start | bytes 786436
